TPU v7x, 256 devices: a whole 4x4x8 slice. The times are simulated.
256 devices in a mesh: region: 32 (over x, z), group: 8 (over y, core).
Axes of the slice: x: 4, y: 4, z: 8, core: 2. Of those that a mesh axis runs over, the one named last changes fastest.
Arguments:
- block_coords: int32 [8, 192, 3], P('group', 'region'), may hold values from -100 to 63, as said below
- features: bfloat16 [8, 192, 8, 8, 8, 128], P('group', 'region'), may hold values from -6 to 6
- cotangent: bfloat16 [8, 192, 4, 4, 4, 128], P('group', 'region'), may hold values from -6 to 6
- weights: bfloat16 [3, 3, 3, 128, 128], replicated, may hold values from -0.109375 to 0.109375
Outputs:
- coarse_features: bfloat16 [8, 192, 4, 4, 4, 128], P('group', 'region')
- grad_features: bfloat16 [8, 192, 8, 8, 8, 128], P('group', 'region')
- grad_weight: float32 [3, 3, 3, 128, 128], replicated
Inputs may be any that keep to these rules, and one draw needn't show every extreme that they name: `block_coords`: slot s of device r along region holds a block with coordinates (x, y, z), x being 2r or 2r+1, 0 <= y < 1, 0 <= z < 4; a device's blocks are distinct; its occupied slots come first and the others hold -100 in all three coordinates; every device holds 3 to 6 blocks, and in each map one device holds 6 and another 6 // 2.
All inputs are finite; a program needn't handle non-finite values.
Results may differ from a plain program's by a relative error of at most 0.0023.
Values may be sent and summed in bfloat16 or wider, within the bound.
No kernel may reach another device: no remote copies, remote signals or barrier semaphores. Data moves between devices by JAX's collectives and lax.ppermute only.
A program may use at most 64 MiB of HBM per device.

v0:
```python
import math
import jax
import jax.numpy as jnp
from jax import lax
from jax.sharding import PartitionSpec as P

CROSS_Y = 1
CROSS_Z = 4
LOWER_SIDES = (
    (-1, 0, 0),
    (-1, -1, 0),
    (-1, 0, -1),
    (-1, -1, -1),
    (0, -1, 0),
    (0, 0, -1),
    (0, -1, -1),
)


def shifted(block, axis, distance):
    devices = range(lax.axis_size(axis))
    route = [(i - distance, i) for i in devices if i - distance in devices]
    return lax.ppermute(block, axis, route)


def unfold(volume, which_axis):
    pieces = [lax.slice_in_dim(volume, offset, offset + 7, 2, which_axis) for offset in range(3)]
    return jnp.stack(pieces, axis=which_axis + 1)


def fold_back(col_terms, which_axis):
    lower_part, middle_part, upper_part = [
        lax.index_in_dim(col_terms, offset, which_axis + 1, keepdims=False) for offset in range(3)
    ]
    zero_row = jnp.zeros_like(lax.slice_in_dim(lower_part, 0, 1, 1, which_axis))
    even_rows = jnp.concatenate([lower_part, zero_row], which_axis) + jnp.concatenate(
        [zero_row, upper_part], which_axis
    )
    paired = jnp.stack(
        [lax.slice_in_dim(even_rows, 0, 4, 1, which_axis), middle_part], which_axis + 1
    )
    new_shape = list(lower_part.shape)
    new_shape[which_axis] = 8
    merged = paired.reshape(new_shape)
    return jnp.concatenate([merged, lax.slice_in_dim(even_rows, 4, 5, 1, which_axis)], which_axis)


def pick_rows(lookup_table, link):
    safe_rows = jnp.clip(link[0], 0, lookup_table.shape[0] - 1)
    gathered = jnp.take(lookup_table, safe_rows, axis=0)
    present_mask = link[1].reshape((-1,) + (1,) * (gathered.ndim - 1))
    return jnp.where(present_mask, gathered, jnp.zeros_like(gathered))


def assemble(blocks, planes, source_links):
    face_x = pick_rows(planes, source_links[0])
    edge_xy = pick_rows(planes[:, 7], source_links[1])
    edge_xz = pick_rows(planes[:, :, 7], source_links[2])
    corner = pick_rows(planes[:, 7, 7], source_links[3])
    face_y = pick_rows(blocks[:, :, 7], source_links[4])
    face_z = pick_rows(blocks[:, :, :, 7], source_links[5])
    edge_yz = pick_rows(blocks[:, :, 7, 7], source_links[6])
    first_plane = jnp.concatenate(
        [
            jnp.concatenate([corner[:, None, None], edge_xy[:, None]], axis=2),
            jnp.concatenate([edge_xz[:, :, None], face_x], axis=2),
        ],
        axis=1,
    )
    low_row = jnp.concatenate([edge_yz[:, :, None], face_y], axis=2)[:, :, None]
    interior = jnp.concatenate([face_z[:, :, :, None], blocks], axis=3)
    upper_part = jnp.concatenate([low_row, interior], axis=2)
    return jnp.concatenate([first_plane[:, None], upper_part], axis=1)


def aim_rows(link, limit):
    return jnp.where(link[1], link[0], limit)


def spread_rims(ext_grads, source_links, block_count, table_rows):
    own_grad = ext_grads[:, 1:, 1:, 1:]
    planes = jnp.zeros((table_rows,) + own_grad.shape[2:], ext_grads.dtype)
    planes = planes.at[aim_rows(source_links[0], table_rows)].add(
        ext_grads[:, 0, 1:, 1:], mode="drop"
    )
    planes = planes.at[aim_rows(source_links[1], table_rows), 7].add(
        ext_grads[:, 0, 0, 1:], mode="drop"
    )
    planes = planes.at[aim_rows(source_links[2], table_rows), :, 7].add(
        ext_grads[:, 0, 1:, 0], mode="drop"
    )
    planes = planes.at[aim_rows(source_links[3], table_rows), 7, 7].add(
        ext_grads[:, 0, 0, 0], mode="drop"
    )
    own_grad = own_grad.at[aim_rows(source_links[4], block_count), :, 7].add(
        ext_grads[:, 1:, 0, 1:], mode="drop"
    )
    own_grad = own_grad.at[aim_rows(source_links[5], block_count), :, :, 7].add(
        ext_grads[:, 1:, 1:, 0], mode="drop"
    )
    own_grad = own_grad.at[aim_rows(source_links[6], block_count), :, 7, 7].add(
        ext_grads[:, 1:, 0, 0], mode="drop"
    )
    return (own_grad, planes)


def find_links(coords, region_rank, block_count):
    slot_ids = jnp.arange(block_count, dtype=jnp.int32)
    collected = []
    for side in LOWER_SIDES:
        wanted = coords + jnp.array(side, jnp.int32)
        matches = jnp.all(wanted[:, None, :] == coords[None, :, :], axis=2)
        present = jnp.any(matches, axis=1)
        source = jnp.sum(jnp.where(matches, slot_ids[None, :], 0), axis=1)
        if side[0] == -1:
            remote = (
                (wanted[:, 0] == 2 * region_rank - 1)
                & (wanted[:, 1] >= 0)
                & (wanted[:, 1] < CROSS_Y)
                & (wanted[:, 2] >= 0)
                & (wanted[:, 2] < CROSS_Z)
            )
            source = jnp.where(present, source, block_count + wanted[:, 1] * CROSS_Z + wanted[:, 2])
            present = present | remote
        collected.append((source, present))
    return collected


def per_device(block_coords, features, cotangent, weights):
    coords = block_coords[0]
    blocks = features[0]
    upstream = cotangent[0]
    block_count = blocks.shape[0]
    cell_count = CROSS_Y * CROSS_Z
    region_rank = lax.axis_index("region")
    occupied = coords[:, 0] >= 0
    cell_index = coords[:, 1] * CROSS_Z + coords[:, 2]
    in_top = coords[:, 0] == 2 * region_rank + 1
    top_planes = blocks[:, 7]
    outgoing = (
        jnp.zeros((cell_count,) + top_planes.shape[1:], blocks.dtype)
        .at[jnp.where(in_top, cell_index, cell_count)]
        .set(top_planes, mode="drop")
    )
    incoming = shifted(outgoing, "region", 1)
    source_links = find_links(coords, region_rank, block_count)
    plane_table = jnp.concatenate([top_planes, incoming], axis=0)
    extended = assemble(blocks, plane_table, source_links)
    columns = unfold(unfold(unfold(extended, 1), 3), 5)
    block_mask = occupied[:, None, None, None, None]
    result = jnp.einsum(
        "nxaybzcf,abcfo->nxyzo", columns, weights, preferred_element_type=jnp.float32
    )
    coarse = jnp.where(block_mask, result, 0.0).astype(jnp.bfloat16)
    masked = jnp.where(block_mask, upstream, jnp.zeros_like(upstream))
    local_grad = jnp.einsum(
        "nxaybzcf,nxyzo->abcfo", columns, masked, preferred_element_type=jnp.float32
    )
    col_terms = jnp.einsum(
        "nxyzo,abcfo->nxaybzcf", masked, weights, preferred_element_type=jnp.float32
    )
    ext_grads = fold_back(fold_back(fold_back(col_terms, 5), 3), 1)
    own_grad, plane_grads = spread_rims(
        ext_grads, source_links, block_count, block_count + cell_count
    )
    own_grad = own_grad.at[:, 7].add(plane_grads[:block_count])
    returned = shifted(plane_grads[block_count:].astype(jnp.bfloat16), "region", -1).astype(
        jnp.float32
    )
    own_grad = own_grad.at[:, 7].add(pick_rows(returned, (cell_index, in_top)))
    summed = lax.psum(local_grad, ("region", "group"))
    grad_scale = 1.0 / math.sqrt(
        lax.axis_size("group") * lax.axis_size("region") * block_count * upstream.shape[1] ** 3
    )
    return (coarse[None], own_grad.astype(jnp.bfloat16)[None], summed * grad_scale)


def solution(mesh):
    return jax.shard_map(
        per_device,
        mesh=mesh,
        in_specs=(
            P("group", "region", None),
            P("group", "region", None, None, None, None),
            P("group", "region", None, None, None, None),
            P(),
        ),
        out_specs=(
            P("group", "region", None, None, None, None),
            P("group", "region", None, None, None, None),
            P(),
        ),
        check_vma=False,
    )
```

profile of v0, /device:TPU:2, one launch (start us, length us, event | category | flops | bytes accessed | tf_op | source)
XLA Modules:
  0.0 414.1 jit_solution(1295653864026888875)
XLA Ops:
  8.5 1.8 convolution_bitcast_fusion
  12.2 1.8 copy.118
  14.1 2.3 copy_dynamic-update-slice_fusion
  16.8 15.9 %dynamic-update-slice.7 = f32[6,4,3,4,3,9,128]{6,5,3,1,0,2,4:T(8,128)} dynamic-update-slice(f32[6,4,3,4,3,9,128]{6,5,3,1,0,2,4:T(8,128)} %copy_dynamic-update-slice_fusion, f32[6,4,3,4,3,1,128]{6,5,3,1,0,2,4:T(1,128)S(1)} %copy.120, s32[]{} %constant.354, s32[]{} %constant.354, s32[]{} %constant.354, s32[]{} %constant.354, s32[]{} %constant.354, s32[]{} %constant.355, s32[]{} %constant.354) | dynamic-update-slice | bytes 884740 | tf_op jit(solution)/shard_map/concatenate | solution.py:45
  32.7 3.8 fusion.70
  36.5 1.7 fusion.4
  40.4 2.2 pad_maximum_fusion.1
  42.6 2.5 copy.121
  59.1 7.7 %collective-permute-start.1 = (bf16[4,8,8,128]{3,2,1,0:T(8,128)(2,1)}, bf16[4,8,8,128]{3,2,1,0:T(8,128)(2,1)}, u32[]{:S(2)}, u32[]{:S(2)}) collective-permute-start(bf16[4,8,8,128]{3,2,1,0:T(8,128)(2,1)} %slice.526), channel_id=1, source_target_pairs={{8,0},{16,8},{24,16},{32,24},{40,32},{48,40},{56,48},{64,56},{72,6... | collective-permute-start | bytes 196616 | tf_op jit(solution)/shard_map/ppermute | solution.py:23
  66.8 2.1 copy.186
  72.1 2.1 collective-permute-start
  87.9 1.8 scatter_fusion.1
  91.8 2.4 scatter_fusion.2
  94.2 2.3 copy.126
  108.2 2.2 gather_fusion.6
  110.4 1.6 fusion.27
  115.8 2.1 gather_fusion.7
  127.6 2.1 gather_fusion.1
  139.8 4.0 convolution_bitcast_fusion.1
  146.0 3.8 scatter-add.66
  149.8 3.8 scatter-add.67
  156.0 2.4 fusion.16
  159.0 245.4 %all-reduce.14.cloned.1.call-done = f32[3,3,3,128,128]{4,3,2,1,0:T(8,128)} async-done(((f32[3,3,3,128,128]{4,3,2,1,0:T(8,128)}), f32[3,3,3,128,128]{4,3,2,1,0:T(8,128)}) %all-reduce.14.cloned.1.call-update) | async-done | bytes 1769488 | tf_op jit(solution)/shard_map/psum | solution.py:171
  404.4 2.9 broadcast_multiply_fusion
  (206 shorter events, 78.5 us)
Async XLA Ops:
  7.2 397.2 %all-reduce.14.cloned.1.call-start = ((), (), s32[]{:S(2)}) async-start(), calls=%async_computation | async-start | bytes 3538944 | tf_op jit(solution)/shard_map/psum | solution.py:171
  8.5 1.8 copy-start.20
  39.3 16.9 %copy-start.19 = (s32[6,3]{0,1:T(4,128)}, s32[6,3]{0,1:T(4,128)S(1)}, u32[]{:S(2)}) copy-start(s32[6,3]{0,1:T(4,128)S(1)} %get-tuple-element.88) | copy-start | bytes 220
  40.2 13.6 %copy-start.29 = (pred[6]{0:T(512)(128)(4,1)}, pred[6]{0:T(512)(128)(4,1)S(1)}, u32[]{:S(2)}) copy-start(pred[6]{0:T(512)(128)(4,1)S(1)} %reduce_or.75) | copy-start | bytes 22
  51.2 2.1 copy-start.23
  51.3 3.9 copy-start.30
  52.4 17.5 %copy-start.24 = (pred[6]{0:T(512)(128)(4,1)}, pred[6]{0:T(512)(128)(4,1)S(1)}, u32[]{:S(2)}) copy-start(pred[6]{0:T(512)(128)(4,1)S(1)} %reduce_or.74) | copy-start | bytes 22
  52.5 17.4 %copy-start.31 = (s32[6]{0:T(128)}, s32[6]{0:T(128)S(1)}, u32[]{:S(2)}) copy-start(s32[6]{0:T(128)S(1)} %select_reduce_fusion.4) | copy-start | bytes 76
  59.1 84.8 %collective-permute-start.1 = (bf16[4,8,8,128]{3,2,1,0:T(8,128)(2,1)}, bf16[4,8,8,128]{3,2,1,0:T(8,128)(2,1)}, u32[]{:S(2)}, u32[]{:S(2)}) collective-permute-start(bf16[4,8,8,128]{3,2,1,0:T(8,128)(2,1)} %slice.526), channel_id=1, source_target_pairs={{8,0},{16,8},{24,16},{32,24},{40,32},{48,40},{56,48},{64,56},{72,6... | collective-permute-start | bytes 196616 | tf_op jit(solution)/shard_map/ppermute | solution.py:23
  71.4 3.5 copy-start.5
  72.1 50.2 %collective-permute-start = (bf16[4,8,8,128]{3,0,2,1:T(4,128)(2,1)}, bf16[4,8,8,128]{3,0,2,1:T(4,128)(2,1)}, u32[]{:S(2)}, u32[]{:S(2)}) collective-permute-start(bf16[4,8,8,128]{3,0,2,1:T(4,128)(2,1)} %copy.94), channel_id=1, source_target_pairs={{0,8},{8,16},{16,24},{24,32},{32,40},{40,48},{48,56},{56,64},{64,7... | collective-permute-start | bytes 196616 | tf_op jit(solution)/shard_map/ppermute | solution.py:23
  77.0 2.3 copy-start.25
  77.0 6.0 %copy-start.33 = (s32[6,1]{0,1:T(1,128)S(1)}, s32[6,1]{0,1:T(1,128)}, u32[]{:S(2)}) copy-start(s32[6,1]{0,1:T(1,128)} %get-tuple-element.51) | copy-start | bytes 76
  77.0 7.1 %copy-start.3 = (bf16[1,6,8,8,8,128]{5,1,4,3,2,0:T(8,128)(2,1)S(1)}, bf16[1,6,8,8,8,128]{5,1,4,3,2,0:T(8,128)(2,1)}, u32[]{:S(2)}) copy-start(bf16[1,6,8,8,8,128]{5,1,4,3,2,0:T(8,128)(2,1)} %copy-done.2) | copy-start | bytes 2359300
  89.7 2.1 copy-start.26
  94.2 12.5 %copy-start.40 = (s32[6]{0:T(128)S(1)}, s32[6]{0:T(128)}, u32[]{:S(2)}) copy-start(s32[6]{0:T(128)} %get-tuple-element.66) | copy-start | bytes 76
  118.8 2.6 copy-start.16
  118.9 3.4 copy-start.32
  133.5 2.3 copy-start.8
  133.5 2.3 copy-start.9
  137.4 2.4 copy-start.18
  137.4 2.4 copy-start.21
  153.6 2.0 copy-start.13
  153.6 2.3 copy-start.15
  (21 other events, 24.9 us)
Sparse Core Ops, SparseCore 0:
  143.9 260.3 all-reduce.13
where the time goes:
time: 416 us; the launch traced here: 414 us
  waiting for transfers between devices  245 us (59%)
  local copies, waits for them, and re-layouts  77.7 us (19%)
  other arithmetic  58.1 us (14%)
  between operations  14.9 us (4%)
  starting transfers between devices  9.9 us (2%)
  matrix products  8.18 us (2%)
    psum x1, waiting for transfers between devices, per_device(): summed = lax.psum(local_grad, ('region', 'group'))  245 us
    concatenate x1, local copies, waits for them, and re-layouts, fold_back(): jnp.concatenate([merged, lax.slice_in_dim(even_rows, 4, 5, 1, which_axis)...  15.9 us
    unnamed x90, local copies, waits for them, and re-layouts  14.1 us
    gather x8, local copies, waits for them, and re-layouts, pick_rows(): gathered = jnp.take(lookup_table, safe_rows, axis=0)  11 us
    ppermute x2, starting transfers between devices, shifted(): return lax.ppermute(block, axis, route)  9.86 us
  transfers between devices with their start and end apart: 3, of which 1 were waited for; matrix products, arithmetic and copies ran while one was open for 21% of the time, Pallas kernels for 0%

commit v1 on v0

--- a/solution.py
+++ b/solution.py
@@ -168,7 +168,9 @@
         jnp.float32
     )
     own_grad = own_grad.at[:, 7].add(pick_rows(returned, (cell_index, in_top)))
-    summed = lax.psum(local_grad, ("region", "group"))
+    summed = local_grad
+    for name in ("region", "group"):
+        summed = lax.psum(summed, name)
     grad_scale = 1.0 / math.sqrt(
         lax.axis_size("group") * lax.axis_size("region") * block_count * upstream.shape[1] ** 3
     )

time: 416 us -> 340 us (0.82)
  waiting for transfers between devices: 245 us -> 174 us
  other arithmetic: 58.1 us -> 51.1 us
    psum x1 -> x2, waiting for transfers between devices: 245 us -> 174 us  [per_device(): summed = lax.psum(summed, name)]
    unnamed x90 -> x110, local copies, waits for them, and re-layouts: 14.1 us -> 16.4 us
  transfers between devices with their start and end apart: 3 -> 4, of which waited for: 1 -> 2; matrix products, arithmetic and copies ran while one was open for 21% -> 30% of each run, Pallas kernels for 0% -> 0%
where the time goes in v1:
time: 340 us; the launch traced here: 339 us
  waiting for transfers between devices  174 us (51%)
  local copies, waits for them, and re-layouts  81.1 us (24%)
  other arithmetic  51.1 us (15%)
  between operations  15 us (4%)
  starting transfers between devices  10.2 us (3%)
  matrix products  7.31 us (2%)
    psum x2, waiting for transfers between devices, per_device(): summed = lax.psum(summed, name)  174 us
    unnamed x110, local copies, waits for them, and re-layouts  16.4 us
    concatenate x1, local copies, waits for them, and re-layouts, fold_back(): jnp.concatenate([merged, lax.slice_in_dim(even_rows, 4, 5, 1, which_axis)...  15.9 us
    ppermute x2, starting transfers between devices, shifted(): return lax.ppermute(block, axis, route)  9.91 us
    gather x8, local copies, waits for them, and re-layouts, pick_rows(): gathered = jnp.take(lookup_table, safe_rows, axis=0)  9.69 us
    another operation x6, other arithmetic, fold_back(): jnp.stack([lax.slice_in_dim(even_rows, 0, 4, 1, which_axis), middle_part]...  8.46 us
    another operation x3, local copies, waits for them, and re-layouts, fold_back(): jnp.stack([lax.slice_in_dim(even_rows, 0, 4, 1, which_axis), middle_part]...  8.18 us
  transfers between devices with their start and end apart: 4, of which 2 were waited for; matrix products, arithmetic and copies ran while one was open for 30% of the time, Pallas kernels for 0%

profile of v1, /device:TPU:2, one launch (start us, length us, event | category | flops | bytes accessed | tf_op | source)
XLA Modules:
  0.0 338.8 jit_solution(14078835009861905952)
XLA Ops:
  9.1 2.1 copy.186
  12.7 3.8 %collective-permute-start = (bf16[4,8,8,128]{3,0,2,1:T(4,128)(2,1)}, bf16[4,8,8,128]{3,0,2,1:T(4,128)(2,1)}, u32[]{:S(2)}, u32[]{:S(2)}) collective-permute-start(bf16[4,8,8,128]{3,0,2,1:T(4,128)(2,1)} %copy.94), channel_id=1, source_target_pairs={{0,8},{8,16},{16,24},{24,32},{32,40},{40,48},{48,56},{56,64},{64,7... | collective-permute-start | bytes 196616 | tf_op jit(solution)/shard_map/ppermute | solution.py:23
  17.5 2.1 slice_bitcast_fusion.2
  19.6 1.7 fusion.2
  30.2 2.9 pad_maximum_fusion
  33.1 1.8 copy.118
  34.9 2.4 copy_dynamic-update-slice_fusion
  37.8 15.9 %dynamic-update-slice.7 = f32[6,4,3,4,3,9,128]{6,5,3,1,0,2,4:T(8,128)} dynamic-update-slice(f32[6,4,3,4,3,9,128]{6,5,3,1,0,2,4:T(8,128)} %copy_dynamic-update-slice_fusion, f32[6,4,3,4,3,1,128]{6,5,3,1,0,2,4:T(1,128)S(1)} %copy.120, s32[]{} %constant.354, s32[]{} %constant.354, s32[]{} %constant.354, s32[]{} %constant.354, s32[]{} %constant.354, s32[]{} %constant.355, s32[]{} %constant.354) | dynamic-update-slice | bytes 884740 | tf_op jit(solution)/shard_map/concatenate | solution.py:45
  53.7 6.4 %fusion.70 = (f32[6,4,3,4,1,9,128]{6,5,3,1,0,2,4:T(8,128)}, f32[6,4,3,4,9,128]{5,4,3,1,0,2:T(8,128)S(1)}, f32[6,4,3,4,9,128]{5,4,3,1,0,2:T(8,128)}) fusion(f32[6,4,3,4,3,9,128]{6,5,3,1,0,2,4:T(8,128)} %dynamic-update-slice.7), kind=kLoop, calls=%fused_computation.249 | loop fusion | bytes 7962624 | tf_op jit(solution)/shard_map/slice | solution.py:33
  71.3 2.1 gather_fusion.7
  79.1 3.0 pad_maximum_fusion.1
  88.5 2.2 gather_fusion.1
  101.2 4.0 %convolution_bitcast_fusion.1 = f32[3,3,3,128,128]{4,3,2,1,0:T(8,128)} fusion(bf16[6,4,3,4,3,4,1,128]{7,0,6,4,2,5,3,1:T(8,128)(2,1)S(1)} %get-tuple-element.76, bf16[6,4,3,4,3,4,1,128]{7,0,6,4,2,5,3,1:T(8,128)(2,1)S(1)} %get-tuple-element.77, bf16[6,4,3,4,3,4,1,128]{7,0,6,4,2,5,3,1:T(8,128)(2,1)S(1)} %get-tuple-element.75, ...), kind=kOutput, calls=%fused_computation.57 | convolution fusion | flops 342441984 | bytes 4521990 | tf_op jit(solution)/shard_map/nxaybzcf,nxyzo->abcfo/dot_general | solution.py:156
  105.6 4.8 %copy.121 = f32[6,4,3,4,2,9,128]{6,4,3,5,2,1,0:T(2,128)S(1)} copy(f32[6,4,3,4,2,9,128]{6,5,3,1,0,2,4:T(8,128)} %pad_maximum_fusion.1) | data formatting | bytes 5308416 | tf_op jit(solution)/shard_map/stack | solution.py:39
  119.8 6.1 %collective-permute-start.1 = (bf16[4,8,8,128]{3,2,1,0:T(8,128)(2,1)S(1)}, bf16[4,8,8,128]{3,2,1,0:T(8,128)(2,1)S(1)}, u32[]{:S(2)}, u32[]{:S(2)}) collective-permute-start(bf16[4,8,8,128]{3,2,1,0:T(8,128)(2,1)S(1)} %slice.526), channel_id=1, source_target_pairs={{8,0},{16,8},{24,16},{32,24},{40,32},{48,40},{56,48},{64,56},{72,6... | collective-permute-start | bytes 196616 | tf_op jit(solution)/shard_map/ppermute | solution.py:23
  125.9 2.2 copy.124
  134.4 2.3 scatter_fusion.2
  136.7 2.3 copy.126
  141.5 116.9 %all-reduce.15.cloned.1.call-done = f32[3,3,3,128,128]{4,3,2,1,0:T(8,128)} async-done(((f32[3,3,3,128,128]{4,3,2,1,0:T(8,128)}), f32[3,3,3,128,128]{4,3,2,1,0:T(8,128)}) %all-reduce.15.cloned.1.call-update) | async-done | bytes 1769488 | tf_op jit(solution)/shard_map/psum | solution.py:173
  259.0 3.8 %scatter-add.66 = f32[6,8,8,8,128]{4,1,3,2,0:T(8,128)S(1)} dynamic-update-slice(f32[6,8,8,8,128]{4,1,3,2,0:T(8,128)S(1)} %scatter_fusion.3, f32[6,1,8,8,128]{4,1,3,2,0:T(1,128)S(1)} %get-tuple-element.46, s32[]{:T(128)} %constant.164.clone.1, s32[]{:T(128)} %constant.180.clone.1, s32[]{:T(128)} %constant.164.clone.1, s32[]{:T(128)} %constant.164.clone.1, s32[]{:T(128)} %constant.164.clone.1) | dynamic-update-slice | bytes 393220 | tf_op jit(solution)/shard_map/scatter-add | solution.py:166
  262.8 3.8 %scatter-add.67 = f32[6,8,8,8,128]{4,1,3,2,0:T(8,128)S(1)} dynamic-update-slice(f32[6,8,8,8,128]{4,1,3,2,0:T(8,128)S(1)} %scatter-add.66, f32[6,1,8,8,128]{4,1,3,2,0:T(1,128)S(1)} %get-tuple-element.45, s32[]{:T(128)} %constant.164.clone.1, s32[]{:T(128)} %constant.180.clone.1, s32[]{:T(128)} %constant.164.clone.1, s32[]{:T(128)} %constant.164.clone.1, s32[]{:T(128)} %constant.164.clone.1) | dynamic-update-slice | bytes 393220 | tf_op jit(solution)/shard_map/scatter-add | solution.py:170
  268.9 2.4 fusion.16
  271.9 57.1 %all-reduce.17.cloned.1.call-done = f32[3,3,3,128,128]{4,3,2,1,0:T(8,128)} async-done(((f32[3,3,3,128,128]{4,3,2,1,0:T(8,128)}), f32[3,3,3,128,128]{4,3,2,1,0:T(8,128)}) %all-reduce.17.cloned.1.call-update) | async-done | bytes 1769488 | tf_op jit(solution)/shard_map/psum | solution.py:173
  329.1 2.9 broadcast_multiply_fusion
  (229 shorter events, 68.7 us)
Async XLA Ops:
  7.2 9.4 %copy-start = (bf16[3,3,3,128,128]{4,3,2,1,0:T(8,128)(2,1)S(1)}, bf16[3,3,3,128,128]{4,3,2,1,0:T(8,128)(2,1)}, u32[]{:S(2)}) copy-start(bf16[3,3,3,128,128]{4,3,2,1,0:T(8,128)(2,1)} %param.22) | copy-start | bytes 2654212
  7.2 9.4 %copy-start.18 = (bf16[1,6,4,4,4,128]{5,4,3,2,1,0:T(4,128)(2,1)S(1)}, bf16[1,6,4,4,4,128]{5,4,3,2,1,0:T(4,128)(2,1)}, u32[]{:S(2)}) copy-start(bf16[1,6,4,4,4,128]{5,4,3,2,1,0:T(4,128)(2,1)} %param.21) | copy-start | bytes 294916
  7.2 251.2 %all-reduce.15.cloned.1.call-start = ((), (), s32[]{:S(2)}) async-start(), calls=%async_computation | async-start | bytes 3538944 | tf_op jit(solution)/shard_map/psum | solution.py:173
  8.6 8.9 %copy-start.24 = (pred[6]{0:T(512)(128)(4,1)}, pred[6]{0:T(512)(128)(4,1)S(1)}, u32[]{:S(2)}) copy-start(pred[6]{0:T(512)(128)(4,1)S(1)} %get-tuple-element.84) | copy-start | bytes 22
  11.2 18.9 %copy-start.5 = (bf16[1,6,8,8,8,128]{5,1,4,3,2,0:T(8,128)(2,1)}, bf16[1,6,8,8,8,128]{5,1,4,3,2,0:T(8,128)(2,1)S(1)}, u32[]{:S(2)}) copy-start(bf16[1,6,8,8,8,128]{5,1,4,3,2,0:T(8,128)(2,1)S(1)} %copy.186) | copy-start | bytes 2359300
  12.7 70.0 %collective-permute-start = (bf16[4,8,8,128]{3,0,2,1:T(4,128)(2,1)}, bf16[4,8,8,128]{3,0,2,1:T(4,128)(2,1)}, u32[]{:S(2)}, u32[]{:S(2)}) collective-permute-start(bf16[4,8,8,128]{3,0,2,1:T(4,128)(2,1)} %copy.94), channel_id=1, source_target_pairs={{0,8},{8,16},{16,24},{24,32},{32,40},{40,48},{48,56},{56,64},{64,7... | collective-permute-start | bytes 196616 | tf_op jit(solution)/shard_map/ppermute | solution.py:23
  22.5 7.6 %copy-start.33 = (pred[6]{0:T(512)(128)(4,1)}, pred[6]{0:T(512)(128)(4,1)S(1)}, u32[]{:S(2)}) copy-start(pred[6]{0:T(512)(128)(4,1)S(1)} %reduce_or.75) | copy-start | bytes 22
  25.9 47.6 %copy-start.27 = (pred[6]{0:T(512)(128)(4,1)}, pred[6]{0:T(512)(128)(4,1)S(1)}, u32[]{:S(2)}) copy-start(pred[6]{0:T(512)(128)(4,1)S(1)} %reduce_or.79) | copy-start | bytes 22
  53.7 6.4 %copy-start.51 = (s32[6]{0:T(128)S(1)}, s32[6]{0:T(128)}, u32[]{:S(2)}) copy-start(s32[6]{0:T(128)} %select_reduce_fusion.2) | copy-start | bytes 76
  53.7 7.5 %copy-start.35 = (s32[6]{0:T(128)S(1)}, s32[6]{0:T(128)}, u32[]{:S(2)}) copy-start(s32[6]{0:T(128)} %select_reduce_fusion.5) | copy-start | bytes 76
  53.7 8.2 %copy-start.36 = (s32[6]{0:T(128)S(1)}, s32[6]{0:T(128)}, u32[]{:S(2)}) copy-start(s32[6]{0:T(128)} %select_reduce_fusion.4) | copy-start | bytes 76
  53.7 10.5 %copy-start.46 = (s32[6]{0:T(128)S(1)}, s32[6]{0:T(128)}, u32[]{:S(2)}) copy-start(s32[6]{0:T(128)} %fusion.68) | copy-start | bytes 76
  53.7 11.1 %copy-start.34 = (pred[6]{0:T(512)(128)(4,1)S(1)}, pred[6]{0:T(512)(128)(4,1)}, u32[]{:S(2)}) copy-start(pred[6]{0:T(512)(128)(4,1)} %copy-done.33) | copy-start | bytes 22
  53.7 11.1 %copy-start.39 = (pred[6,1]{0,1:T(4,128)(4,1)S(1)}, pred[6,1]{0,1:T(4,128)(4,1)}, u32[]{:S(2)}) copy-start(pred[6,1]{0,1:T(4,128)(4,1)} %get-tuple-element.103) | copy-start | bytes 22
  53.7 11.7 %copy-start.49 = (s32[6]{0:T(128)S(1)}, s32[6]{0:T(128)}, u32[]{:S(2)}) copy-start(s32[6]{0:T(128)} %get-tuple-element.105) | copy-start | bytes 76
  53.7 12.2 %copy-start.17 = (bf16[6,8,8,128]{3,0,2,1:T(8,128)(2,1)S(1)}, bf16[6,8,8,128]{3,0,2,1:T(8,128)(2,1)}, u32[]{:S(2)}) copy-start(bf16[6,8,8,128]{3,0,2,1:T(8,128)(2,1)} %slice_bitcast_fusion.14) | copy-start | bytes 294916
  53.7 12.9 %copy-start.47 = (s32[6]{0:T(128)S(1)}, s32[6]{0:T(128)}, u32[]{:S(2)}) copy-start(s32[6]{0:T(128)} %get-tuple-element.104) | copy-start | bytes 76
  105.3 223.8 %all-reduce.17.cloned.1.call-start = ((), (), s32[]{:S(2)}) async-start(), calls=%async_computation.1 | async-start | bytes 3538944 | tf_op jit(solution)/shard_map/psum | solution.py:173
  113.4 3.7 %copy-start.23 = (s32[6]{0:T(128)S(1)}, s32[6]{0:T(128)}, u32[]{:S(2)}) copy-start(s32[6]{0:T(128)} %get-tuple-element.54) | copy-start | bytes 76
  113.4 4.6 %copy-start.22 = (s32[6]{0:T(128)S(1)}, s32[6]{0:T(128)}, u32[]{:S(2)}) copy-start(s32[6]{0:T(128)} %get-tuple-element.52) | copy-start | bytes 76
  114.9 4.0 %copy-start.20 = (s32[6]{0:T(128)S(1)}, s32[6]{0:T(128)}, u32[]{:S(2)}) copy-start(s32[6]{0:T(128)} %get-tuple-element.49) | copy-start | bytes 76
  119.8 21.2 %collective-permute-start.1 = (bf16[4,8,8,128]{3,2,1,0:T(8,128)(2,1)S(1)}, bf16[4,8,8,128]{3,2,1,0:T(8,128)(2,1)S(1)}, u32[]{:S(2)}, u32[]{:S(2)}) collective-permute-start(bf16[4,8,8,128]{3,2,1,0:T(8,128)(2,1)S(1)} %slice.526), channel_id=1, source_target_pairs={{8,0},{16,8},{24,16},{32,24},{40,32},{48,40},{56,48},{64,56},{72,6... | collective-permute-start | bytes 196616 | tf_op jit(solution)/shard_map/ppermute | solution.py:23
  139.1 119.4 %copy-start.30 = (pred[6]{0:T(512)(128)(4,1)S(1)}, pred[6]{0:T(512)(128)(4,1)}, u32[]{:S(2)}) copy-start(pred[6]{0:T(512)(128)(4,1)} %get-tuple-element.47) | copy-start | bytes 22
  139.1 119.4 %copy-start.31 = (pred[6]{0:T(512)(128)(4,1)S(1)}, pred[6]{0:T(512)(128)(4,1)}, u32[]{:S(2)}) copy-start(pred[6]{0:T(512)(128)(4,1)} %get-tuple-element.83) | copy-start | bytes 22
  (32 other events, 51.9 us)
Sparse Core Ops, SparseCore 0:
  105.4 153.0 all-reduce.14
  260.9 68.0 all-reduce.16
